TPU v7x, 32 devices: a whole 2x2x4 slice. The times are simulated.
32 devices in a mesh: pts: 8 (over y, x, core), lst: 4 (over z).
Axes of the slice: x: 2, y: 2, z: 4, core: 2. Of those that a mesh axis runs over, the one named last changes fastest.
Arguments:
- tower_out: bfloat16 [16384, 1024], P('pts', 'lst'), may hold values from -6 to 6
- projection: bfloat16 [1024, 256], P('lst'), may hold values from -1 to 1
- centroids: bfloat16 [16384, 256], P('lst'), may hold values from -6 to 6
Outputs:
- new_centroids: float32 [16384, 256], P(('lst', 'pts'))
- row_log: float32 [16384], P('pts')
All inputs are finite; a program needn't handle non-finite values.
Results may differ from a plain program's by a relative error of at most 0.0045.
Values may be sent and summed in bfloat16 or wider, within the bound.
A program may use at most 64 MiB of HBM per device.

v0:
```python
import functools
import math

import jax
import jax.numpy as jnp
from jax import lax
from jax.experimental import pallas as pl
from jax.experimental.pallas import tpu as pltpu
from jax.sharding import PartitionSpec as P

ITERS = 3
temper = 0.05
LANES = 128
MESH = pl.DeviceIdType.MESH
F32 = jnp.float32
BF16 = jnp.bfloat16


def rms_norm(values):
    return values * lax.rsqrt(jnp.mean(values * values, axis=-1, keepdims=True) + 1e-06)


def column_of(row, rows):
    return jnp.broadcast_to(row, (rows, LANES)).T


def kernel(
    npts,
    nlst,
    chunks,
    tower,
    proj,
    cent,
    out,
    row_log,
    energy,
    unit,
    full,
    pfull,
    normed,
    lane_sums,
    col_sums,
    row_sums,
    col_wide,
    scaled,
    pair_send,
    pair_recv,
    chip_send,
    chip_recv,
    mine,
    t_send,
    t_recv,
    p_send,
    p_recv,
    q_send,
    q_recv,
    n_send,
    n_recv,
    c_send,
    c_recv,
    r_send,
    r_recv,
    x_send,
    x_recv,
    y_send,
    y_recv,
):
    pts = lax.axis_index("pts")
    lst = lax.axis_index("lst")
    lists, dp = cent.shape
    points = tower.shape[0]
    share = points // nlst
    own = lists // npts
    chips = npts // 2
    core = pts % 2
    chip = pts // 2
    balance = (points * npts) / (lists * nlst)
    list_blocks = lists // LANES
    point_blocks = points // LANES

    barrier = pltpu.get_barrier_semaphore()
    for d in range(1, nlst):
        pl.semaphore_signal(
            barrier, inc=1, device_id={"lst": (lst + d) % nlst}, device_id_type=MESH
        )
    for d in range(1, npts):
        pl.semaphore_signal(
            barrier, inc=1, device_id={"pts": (pts + d) % npts}, device_id_type=MESH
        )
    pl.semaphore_wait(barrier, nlst + npts - 2)

    pending = []

    def send(src, dst, send_sem, recv_sem, axis, target):
        copy = pltpu.make_async_remote_copy(
            src_ref=src,
            dst_ref=dst,
            send_sem=send_sem,
            recv_sem=recv_sem,
            device_id={axis: target},
            device_id_type=MESH,
        )
        copy.start()
        pending.append(copy)
        return copy

    feats = proj.shape[0]
    piece = feats // npts
    sliced = piece % 16 == 0
    if sliced:
        piece_rows = pl.ds(pl.multiple_of(pts * piece, piece), piece)
    else:
        piece_rows = pl.ds(0, feats)
    p_copies = [
        send(
            proj.at[piece_rows],
            pfull.at[d, piece_rows],
            p_send.at[d],
            p_recv.at[d],
            "lst",
            (lst + d) % nlst,
        )
        for d in range(1, nlst)
    ]
    chunk = share // chunks
    t_copies = []
    for c in range(chunks):
        for d in range(1, nlst):
            z = (lst + d) % nlst
            t_copies.append(
                send(
                    tower.at[pl.ds(pl.multiple_of(z * share + c * chunk, chunk), chunk)],
                    full.at[c, d],
                    t_send.at[c, d],
                    t_recv.at[c, d],
                    "lst",
                    z,
                )
            )
    unit_rows = min(256, lists)

    @pl.loop(0, lists // unit_rows)
    def _(b):
        rows = pl.ds(pl.multiple_of(b * unit_rows, unit_rows), unit_rows)
        unit[rows, :] = rms_norm(cent[rows, :].astype(F32)).astype(BF16)
        lane_sums[rows, :] = jnp.zeros((unit_rows, LANES), F32)

    for copy in p_copies:
        copy.wait_recv()
    if sliced:
        q_copies = [
            send(
                pfull.at[pl.ds(1, nlst - 1), piece_rows],
                pfull.at[pl.ds(1, nlst - 1), piece_rows],
                q_send.at[d],
                q_recv.at[d],
                "pts",
                (pts + d) % npts,
            )
            for d in range(1, npts)
        ]

    if sliced:
        for copy in q_copies:
            copy.wait_recv()

    def hop(c, origin, left):
        side = 0 if left else 1
        return pltpu.make_async_remote_copy(
            src_ref=normed.at[c, origin],
            dst_ref=normed.at[c, origin],
            send_sem=n_send.at[side, c, origin],
            recv_sem=n_recv.at[c, origin],
            device_id={"lst": lst - 1 if left else lst + 1},
            device_id_type=MESH,
        )

    has_left = lst > 0
    has_right = lst < nlst - 1
    for c in range(chunks):
        hidden = jnp.dot(
            tower[pl.ds(pl.multiple_of(lst * share + c * chunk, chunk), chunk), :],
            proj[...],
            preferred_element_type=F32,
        )
        for d in range(1, nlst):
            t_copies[c * (nlst - 1) + d - 1].wait_recv()
            hidden += jnp.dot(full[c, d], pfull[d], preferred_element_type=F32)
        normed[c, lst] = rms_norm(hidden).astype(BF16)

        @pl.when(has_left)
        def _(c=c):
            hop(c, lst, True).start()

        @pl.when(has_right)
        def _(c=c):
            hop(c, lst, False).start()

    log2e = 1.0 / math.log(2.0)
    gain = log2e / (dp * temper)
    shift = -log2e / temper
    e_rows = min(1024, lists)
    step = min(256, chunk)

    def energy_of(c, origin):
        @pl.loop(0, lists // e_rows)
        def _(b):
            rows = pl.ds(pl.multiple_of(b * e_rows, e_rows), e_rows)
            sums = lane_sums[rows, :]
            for k in range(chunk // step):
                scores = lax.dot_general(
                    unit[rows, :],
                    normed[c, origin, k * step : (k + 1) * step, :],
                    (((1,), (1,)), ((), ())),
                    preferred_element_type=F32,
                )
                block = jnp.exp2(scores * gain + shift)
                at = pl.multiple_of(origin * share + c * chunk + k * step, step)
                energy[rows, pl.ds(at, step)] = block
                for m in range(step // LANES):
                    sums += block[:, m * LANES : (m + 1) * LANES]
            lane_sums[rows, :] = sums

    paired = jnp.minimum(lst, nlst - 1 - lst)
    for s in range(nlst):
        near = (s + 1) // 2
        far = s - paired
        in_pairs = lst - near if s % 2 else lst + near
        beyond = jnp.where(has_right & (lst < nlst - 1 - lst), lst + far, lst - far)
        origin = jnp.where(s <= 2 * paired, in_pairs, beyond) if s else lst
        for c in range(chunks):
            if s:
                hop(c, origin, True).wait_recv()

                @pl.when((origin < lst) & has_right)
                def _(c=c, origin=origin):
                    hop(c, origin, False).start()

                @pl.when((origin > lst) & has_left)
                def _(c=c, origin=origin):
                    hop(c, origin, True).start()

            energy_of(c, origin)

    for z in range(nlst):
        for c in range(chunks):

            @pl.when((z <= lst) & has_right)
            def _(c=c, z=z):
                hop(c, z, False).wait_send()

            @pl.when((z >= lst) & has_left)
            def _(c=c, z=z):
                hop(c, z, True).wait_send()

    def lane_dense(sums):
        return jnp.sum(sums.T, axis=0, keepdims=True)

    row_scale = None
    for sweep in range(ITERS):

        @pl.loop(0, list_blocks, unroll=4)
        def _(b, sweep=sweep, row_scale=row_scale):
            rows = pl.ds(pl.multiple_of(b * LANES, LANES), LANES)
            if sweep == 0:
                sums = lane_sums[rows, :]
            else:
                sums = energy[rows, 0:LANES] * row_scale[:, 0:LANES]
                for m in range(1, point_blocks):
                    lanes = slice(m * LANES, (m + 1) * LANES)
                    sums += energy[rows, lanes] * row_scale[:, lanes]
            col_sums[sweep, 0, pl.ds(b, 1), :] = lane_dense(sums)

        copies = [
            send(
                col_sums.at[sweep, 0],
                col_sums.at[sweep, d],
                c_send.at[sweep, d],
                c_recv.at[sweep, d],
                "pts",
                (pts + d) % npts,
            )
            for d in range(1, npts)
        ]
        for copy in copies:
            copy.wait_recv()
        total = col_sums[sweep, 0]
        for d in range(1, npts):
            total += col_sums[sweep, d]
        lane_sums[0:list_blocks, :] = balance / total

        def row_step(b, acc):
            rows = pl.ds(pl.multiple_of(b * LANES, LANES), LANES)
            wide = column_of(lane_sums[pl.ds(b, 1), :], LANES)
            if sweep == ITERS - 1:
                col_wide[rows, :] = wide
            parts = []
            for m in range(point_blocks):
                lanes = slice(m * LANES, (m + 1) * LANES)
                term = energy[rows, lanes] * wide
                parts.append(acc[m] + jnp.sum(term.reshape(LANES // 8, 8, LANES), axis=0))
            return tuple(parts)

        acc = lax.fori_loop(
            0,
            list_blocks,
            row_step,
            tuple(jnp.zeros((8, LANES), F32) for _ in range(point_blocks)),
            unroll=4,
        )
        per_slot = share // LANES
        for d in range(nlst):
            parts = [
                jnp.sum(acc[d * per_slot + m], axis=0, keepdims=True) for m in range(per_slot)
            ]
            row_sums[sweep, 0, d : d + 1, :] = jnp.concatenate(parts, axis=1)
        copies = [
            send(
                row_sums.at[sweep, 0],
                row_sums.at[sweep, d],
                r_send.at[sweep, d],
                r_recv.at[sweep, d],
                "lst",
                (lst + d) % nlst,
            )
            for d in range(1, nlst)
        ]
        for copy in copies:
            copy.wait_recv()
        total = row_sums[sweep, 0]
        for d in range(1, nlst):
            total += row_sums[sweep, d]
        scale = 1.0 / total
        row_scale = jnp.concatenate([scale[d : d + 1, :] for d in range(nlst)], axis=1)
    row_log[...] = jnp.log(scale)

    for m in range(point_blocks):
        d, k = divmod(m * LANES, share)
        wide = column_of(row_scale[:, m * LANES : (m + 1) * LANES], LANES)
        c, k = divmod(k, chunk)
        block = normed[c, d, k : k + LANES, :].astype(F32)
        for h in range(dp // LANES):
            lanes = slice(h * LANES, (h + 1) * LANES)
            scaled[m * LANES : (m + 1) * LANES, lanes] = (block[:, lanes] * wide).astype(BF16)

    tile = min(256, own)

    def partial_sums(owner, store):
        @pl.loop(0, own // tile)
        def _(t):
            rows = pl.ds(pl.multiple_of(owner * own + t * tile, tile), tile)
            store(
                pl.ds(pl.multiple_of(t * tile, tile), tile),
                jnp.dot(energy[rows, :].astype(BF16), scaled[...], preferred_element_type=F32),
            )

    partner = pts + 1 - 2 * core
    x_copies = []
    order = [d % chips for d in range(1, chips + 1)]
    for d in order:

        def to_pair(rows, values, d=d):
            pair_send[d, rows, :] = values.astype(BF16)

        partial_sums(((chip + d) % chips) * 2 + 1 - core, to_pair)
        x_copies.append(
            send(pair_send.at[d], pair_recv.at[d], x_send.at[d], x_recv.at[d], "pts", partner)
        )
    y_copies = []
    for n, d in enumerate(order):

        def to_mine(rows, values):
            mine[rows, :] = values

        owner = ((chip + d) % chips) * 2 + core
        partial_sums(owner, to_mine)
        x_copies[n].wait_recv()
        pair = mine[...] + pair_recv[d].astype(F32)
        if d:
            chip_send[d] = pair.astype(BF16)
            y_copies.append(
                send(chip_send.at[d], chip_recv.at[d], y_send.at[d], y_recv.at[d], "pts", owner)
            )
        else:
            mine[...] = pair
    for copy in y_copies:
        copy.wait_recv()
    sums = mine[...]
    for d in range(1, chips):
        sums += chip_recv[d].astype(F32)
    wide = col_wide[pl.ds(pl.multiple_of(pts * own, own), own), :]
    sums = sums * jnp.concatenate([wide] * (dp // LANES), axis=1)
    out[...] = rms_norm(sums)
    for copy in pending:
        copy.wait_send()


def on_device(npts, nlst, tower_out, projection, centroids):
    points = tower_out.shape[0]
    lists, dp = centroids.shape
    feats = tower_out.shape[1]
    share = points // nlst
    own = lists // npts
    chips = npts // 2
    chunks = 2 if share % (2 * LANES) == 0 else 1
    chunk = share // chunks
    vmem = pl.BlockSpec(memory_space=pltpu.VMEM)
    sem = pltpu.SemaphoreType.DMA
    centers, row_log = pl.pallas_call(
        functools.partial(kernel, npts, nlst, chunks),
        out_shape=(
            jax.ShapeDtypeStruct((own, dp), F32),
            jax.ShapeDtypeStruct((nlst, share), F32),
        ),
        in_specs=[vmem] * 3,
        out_specs=(vmem, vmem),
        scratch_shapes=[
            pltpu.VMEM((lists, points), F32),
            pltpu.VMEM((lists, dp), BF16),
            pltpu.VMEM((chunks, nlst, chunk, feats), BF16),
            pltpu.VMEM((nlst, feats, dp), BF16),
            pltpu.VMEM((chunks, nlst, chunk, dp), BF16),
            pltpu.VMEM((lists, LANES), F32),
            pltpu.VMEM((ITERS, npts, lists // LANES, LANES), F32),
            pltpu.VMEM((ITERS, nlst, nlst, share), F32),
            pltpu.VMEM((lists, LANES), F32),
            pltpu.VMEM((points, dp), BF16),
            pltpu.VMEM((chips, own, dp), BF16),
            pltpu.VMEM((chips, own, dp), BF16),
            pltpu.VMEM((chips, own, dp), BF16),
            pltpu.VMEM((chips, own, dp), BF16),
            pltpu.VMEM((own, dp), F32),
            sem((chunks, nlst)),
            sem((chunks, nlst)),
            sem((nlst,)),
            sem((nlst,)),
            sem((npts,)),
            sem((npts,)),
            sem((2, chunks, nlst)),
            sem((chunks, nlst)),
            sem((ITERS, npts)),
            sem((ITERS, npts)),
            sem((ITERS, nlst)),
            sem((ITERS, nlst)),
            sem((chips,)),
            sem((chips,)),
            sem((chips,)),
            sem((chips,)),
        ],
        compiler_params=pltpu.CompilerParams(
            collective_id=0, has_side_effects=True, vmem_limit_bytes=64000000
        ),
    )(tower_out, projection, centroids)
    return centers, row_log.reshape(points)


def solution(mesh):
    return jax.shard_map(
        functools.partial(on_device, mesh.shape["pts"], mesh.shape["lst"]),
        mesh=mesh,
        in_specs=(P("pts", "lst"), P("lst", None), P("lst", None)),
        out_specs=(P(("lst", "pts"), None), P("pts")),
        check_vma=False,
    )
```

profile of v0, /device:TPU:0, one launch (start us, length us, event | category | flops | bytes accessed | tf_op | source)
XLA Modules:
  0.0 112.7 jit_solution(10440833279488942893)
XLA Ops:
  0.6 108.9 %shard_map.50 = (f32[512,256]{1,0:T(8,128)}, f32[4,512]{1,0:T(4,128)}) custom-call(bf16[2048,256]{1,0:T(8,128)(2,1)} %tower.1, bf16[256,256]{1,0:T(8,128)(2,1)} %proj.1, bf16[4096,256]{1,0:T(8,128)(2,1)} %cent.1), custom_call_target="tpu_custom_call" | custom-call | tf_op jit(solution)/shard_map/pallas_call | solution.py:409
  109.6 1.3 %copy.5 = f32[1,4,4,128]{3,1,2,0:T(4,128)} copy(f32[1,4,4,128]{3,2,1,0:T(4,128)} %bitcast.3) | data formatting | bytes 16384
  110.9 1.9 %copy.7 = f32[512,256]{1,0:T(8,128)} copy(f32[512,256]{1,0:T(8,128)} %get-tuple-element.8) | data formatting | bytes 1048576
where the time goes:
time: 113 us
  Pallas kernels  109 us (96%)
  local copies, waits for them, and re-layouts  3.17 us (3%)
    pallas_call x1, Pallas kernels, on_device(): pl.pallas_call(functools.partial(kernel, npts, nlst, chunks), out_shape=(...  109 us
    unnamed x2, local copies, waits for them, and re-layouts  3.17 us

commit v1 on v0

v1 whole, which is shorter than its diff:
```python
import functools
import math
from types import SimpleNamespace

import jax
import jax.numpy as jnp
from jax import lax
from jax.experimental import pallas as pl
from jax.experimental.pallas import tpu as pltpu
from jax.sharding import PartitionSpec as P

ITERS = 3
temper = 0.05
LANES = 128
MESH = pl.DeviceIdType.MESH
F32 = jnp.float32
BF16 = jnp.bfloat16


def rms_norm(values):
    return values * lax.rsqrt(jnp.mean(values * values, axis=-1, keepdims=True) + 1e-06)


def column_of(row, rows):
    return jnp.broadcast_to(row, (rows, LANES)).T


def halved(values, rows):
    while values.shape[0] > rows:
        n = values.shape[0] // 2
        values = values[:n] + values[n:]
    return values


def added(terms):
    while len(terms) > 1:
        rest = terms[len(terms) // 2 * 2 :]
        terms = [terms[i] + terms[i + 1] for i in range(0, len(terms) - 1, 2)] + rest
    return terms[0]


def block(start, size):
    return pl.ds(pl.multiple_of(start * size, size), size)


def energy_block(s, gain, rows, cols, points):
    scores = lax.dot_general(
        s.unit[rows, :], points, (((1,), (1,)), ((), ())), preferred_element_type=F32
    )
    values = jnp.exp2(scores * gain)
    s.energy[rows, cols] = values.astype(BF16)
    width = values.shape[1] // LANES
    s.lane_sums[rows, :] += added([values[:, m * LANES : (m + 1) * LANES] for m in range(width)])


def unit_lists(s):
    lists = s.unit.shape[0]
    rows_each = min(256, lists)

    @pl.loop(0, lists // rows_each)
    def _(b):
        rows = block(b, rows_each)
        s.unit[rows, :] = rms_norm(s.unit[rows, :].astype(F32)).astype(BF16)
        s.lane_sums[rows, :] = jnp.zeros((rows_each, LANES), F32)


def line_gather(s, lst, gain, loads, arrive):
    points = s.tower.shape[0]
    lists = s.unit.shape[0]
    half = points // 2
    steps = half // LANES
    near = lst // 2
    far = 1 - near
    inner = (lst == 1) | (lst == 2)
    outer = jnp.logical_not(inner)
    inner_of_mine = 1 + near
    outer_of_mine = 3 * near
    other_inner = 2 - near

    def remote(src, dst, send_sem, recv_sem, target):
        return pltpu.make_async_remote_copy(
            src_ref=src,
            dst_ref=dst,
            send_sem=send_sem,
            recv_sem=recv_sem,
            device_id={"lst": target},
            device_id_type=MESH,
        )

    def feed(h, t):
        return remote(s.part.at[h, t], s.fed.at[h, t], s.f_send.at[h, t], s.f_recv.at[h, t], inner_of_mine)

    def cross(t):
        return remote(s.part.at[far, t], s.crossed.at[t], s.x_send.at[t], s.x_recv.at[t], other_inner)

    def back(u, h):
        return remote(
            s.normed.at[u, h], s.normed.at[u, h], s.b_send.at[u, h], s.n_recv.at[u, h], outer_of_mine
        )

    def across(u):
        return remote(
            s.normed.at[u, near], s.normed.at[u, near], s.a_send.at[u], s.n_recv.at[u, near], other_inner
        )

    def arrived(u, h):
        return remote(
            s.normed.at[u, h], s.normed.at[u, h], s.b_send.at[u, h], s.n_recv.at[u, h], other_inner
        )

    loads["proj"].wait()
    loads["tower"].wait()
    arrive()

    @pl.loop(0, steps)
    def _(t):
        for h in (far, near):
            values = jnp.dot(
                s.tower[block(h * steps + t, LANES), :], s.proj[...], preferred_element_type=F32
            )

            @pl.when(outer)
            def _(h=h, values=values):
                s.part[h, t] = values.astype(BF16)
                feed(h, t).start()

            @pl.when(inner)
            def _(h=h, values=values):
                s.own[h, t] = values

    loads["cent"].wait()
    unit_lists(s)
    e_rows = min(2048, lists)

    @pl.loop(0, steps + 2)
    def _(t):
        @pl.when(inner & (t < steps))
        def _():
            feed(far, t).wait_recv()
            s.part[far, t] = (s.own[far, t] + s.fed[far, t].astype(F32)).astype(BF16)
            cross(t).start()

        @pl.when(inner & (t >= 1) & (t <= steps))
        def _():
            u = t - 1
            feed(near, u).wait_recv()
            cross(u).wait_recv()
            hidden = s.own[near, u] + s.fed[near, u].astype(F32) + s.crossed[u].astype(F32)
            s.normed[u, near] = rms_norm(hidden).astype(BF16)
            back(u, near).start()
            across(u).start()

        @pl.when(t >= 2)
        def _():
            u = t - 2

            @pl.when(inner)
            def _():
                arrived(u, far).wait_recv()
                back(u, far).start()

            @pl.when(outer)
            def _():
                arrived(u, near).wait_recv()
                arrived(u, far).wait_recv()

            @pl.loop(0, lists // e_rows)
            def _(b):
                rows = block(b, e_rows)
                pair = s.normed[u].reshape(2 * LANES, s.normed.shape[-1])
                energy_block(s, gain, rows, block(u, 2 * LANES), pair)

    def settle():
        @pl.loop(0, steps)
        def _(t):
            @pl.when(outer)
            def _():
                feed(far, t).wait_send()
                feed(near, t).wait_send()

            @pl.when(inner)
            def _():
                cross(t).wait_send()
                back(t, near).wait_send()
                back(t, far).wait_send()
                across(t).wait_send()

    def points_of(m):
        return s.normed[m // 2, m % 2]

    return settle, points_of, [h * steps + u for u in range(steps) for h in range(2)]


def line_scratch(points, lists, feats, dp):
    half = points // 2
    steps = half // LANES
    sem = pltpu.SemaphoreType.DMA
    return dict(
        own=pltpu.VMEM((2, steps, LANES, dp), F32),
        part=pltpu.VMEM((2, steps, LANES, dp), BF16),
        fed=pltpu.VMEM((2, steps, LANES, dp), BF16),
        crossed=pltpu.VMEM((steps, LANES, dp), BF16),
        normed=pltpu.VMEM((steps, 2, LANES, dp), BF16),
        f_send=sem((2, steps)),
        f_recv=sem((2, steps)),
        x_send=sem((steps,)),
        x_recv=sem((steps,)),
        b_send=sem((steps, 2)),
        a_send=sem((steps,)),
        n_recv=sem((steps, 2)),
    )


def any_gather(s, nlst, npts, lst, pts, send, chunks, gain, loads, arrive):
    points = s.tower.shape[0]
    lists = s.unit.shape[0]
    share = points // nlst
    feats = s.proj.shape[0]
    loads["proj"].wait()
    loads["tower"].wait()
    arrive()
    piece = feats // npts
    sliced = piece % 16 == 0
    piece_rows = block(pts, piece) if sliced else pl.ds(0, feats)
    p_copies = [
        send(
            s.proj.at[piece_rows],
            s.pfull.at[d, piece_rows],
            s.p_send.at[d],
            s.p_recv.at[d],
            "lst",
            (lst + d) % nlst,
        )
        for d in range(1, nlst)
    ]
    chunk = share // chunks
    t_copies = []
    for c in range(chunks):
        for d in range(1, nlst):
            z = (lst + d) % nlst
            t_copies.append(
                send(
                    s.tower.at[block(z * chunks + c, chunk)],
                    s.full.at[c, d],
                    s.t_send.at[c, d],
                    s.t_recv.at[c, d],
                    "lst",
                    z,
                )
            )
    loads["cent"].wait()
    unit_lists(s)

    for copy in p_copies:
        copy.wait_recv()
    if sliced:
        q_copies = [
            send(
                s.pfull.at[pl.ds(1, nlst - 1), piece_rows],
                s.pfull.at[pl.ds(1, nlst - 1), piece_rows],
                s.q_send.at[d],
                s.q_recv.at[d],
                "pts",
                (pts + d) % npts,
            )
            for d in range(1, npts)
        ]
        for copy in q_copies:
            copy.wait_recv()

    def hop(c, origin, left):
        side = 0 if left else 1
        return pltpu.make_async_remote_copy(
            src_ref=s.normed.at[c, origin],
            dst_ref=s.normed.at[c, origin],
            send_sem=s.n_send.at[side, c, origin],
            recv_sem=s.n_recv.at[c, origin],
            device_id={"lst": lst - 1 if left else lst + 1},
            device_id_type=MESH,
        )

    has_left = lst > 0
    has_right = lst < nlst - 1
    for c in range(chunks):
        hidden = jnp.dot(
            s.tower[block(lst * chunks + c, chunk), :], s.proj[...], preferred_element_type=F32
        )
        for d in range(1, nlst):
            t_copies[c * (nlst - 1) + d - 1].wait_recv()
            hidden += jnp.dot(s.full[c, d], s.pfull[d], preferred_element_type=F32)
        s.normed[c, lst] = rms_norm(hidden).astype(BF16)

        @pl.when(has_left)
        def _(c=c):
            hop(c, lst, True).start()

        @pl.when(has_right)
        def _(c=c):
            hop(c, lst, False).start()

    e_rows = min(1024, lists)
    step = min(256, chunk)
    per_share = share // step
    per_chunk = chunk // step

    def energy_of(c, origin):
        @pl.loop(0, lists // e_rows)
        def _(b):
            rows = block(b, e_rows)
            for k in range(per_chunk):
                cols = block(origin * per_share + c * per_chunk + k, step)
                energy_block(s, gain, rows, cols, s.normed[c, origin, k * step : (k + 1) * step, :])

    paired = jnp.minimum(lst, nlst - 1 - lst)
    for n in range(nlst):
        close = (n + 1) // 2
        away = n - paired
        in_pairs = lst - close if n % 2 else lst + close
        beyond = jnp.where(has_right & (lst < nlst - 1 - lst), lst + away, lst - away)
        origin = jnp.where(n <= 2 * paired, in_pairs, beyond) if n else lst
        for c in range(chunks):
            if n:
                hop(c, origin, True).wait_recv()

                @pl.when((origin < lst) & has_right)
                def _(c=c, origin=origin):
                    hop(c, origin, False).start()

                @pl.when((origin > lst) & has_left)
                def _(c=c, origin=origin):
                    hop(c, origin, True).start()

            energy_of(c, origin)

    def settle():
        for z in range(nlst):
            for c in range(chunks):

                @pl.when((z <= lst) & has_right)
                def _(c=c, z=z):
                    hop(c, z, False).wait_send()

                @pl.when((z >= lst) & has_left)
                def _(c=c, z=z):
                    hop(c, z, True).wait_send()

    def points_of(m):
        d, k = divmod(m * LANES, share)
        c, k = divmod(k, chunk)
        return s.normed[c, d, k : k + LANES, :]

    return settle, points_of, list(range(points // LANES))


def any_scratch(points, lists, feats, dp, npts, nlst, chunks):
    chunk = points // nlst // chunks
    sem = pltpu.SemaphoreType.DMA
    return dict(
        full=pltpu.VMEM((chunks, nlst, chunk, feats), BF16),
        pfull=pltpu.VMEM((nlst, feats, dp), BF16),
        normed=pltpu.VMEM((chunks, nlst, chunk, dp), BF16),
        t_send=sem((chunks, nlst)),
        t_recv=sem((chunks, nlst)),
        p_send=sem((nlst,)),
        p_recv=sem((nlst,)),
        q_send=sem((npts,)),
        q_recv=sem((npts,)),
        n_send=sem((2, chunks, nlst)),
        n_recv=sem((chunks, nlst)),
    )


def kernel(npts, nlst, chunks, names, tower, proj, cent, out, row_log, *scratch):
    s = SimpleNamespace(**dict(zip(names, scratch)))
    pts = lax.axis_index("pts")
    lst = lax.axis_index("lst")
    lists, dp = s.unit.shape
    points = s.tower.shape[0]
    own = lists // npts
    chips = npts // 2
    core = pts % 2
    chip = pts // 2
    balance = (points * npts) / (lists * nlst)
    list_blocks = lists // LANES
    point_blocks = points // LANES

    loads = {
        "proj": pltpu.make_async_copy(proj, s.proj, s.load.at[0]),
        "tower": pltpu.make_async_copy(tower, s.tower, s.load.at[1]),
        "cent": pltpu.make_async_copy(cent, s.unit, s.load.at[2]),
    }
    for copy in loads.values():
        copy.start()

    barrier = pltpu.get_barrier_semaphore()
    for d in range(1, nlst):
        pl.semaphore_signal(
            barrier, inc=1, device_id={"lst": (lst + d) % nlst}, device_id_type=MESH
        )
    for d in range(1, npts):
        pl.semaphore_signal(
            barrier, inc=1, device_id={"pts": (pts + d) % npts}, device_id_type=MESH
        )

    def arrive():
        pl.semaphore_wait(barrier, nlst + npts - 2)

    pending = []

    def send(src, dst, send_sem, recv_sem, axis, target):
        copy = pltpu.make_async_remote_copy(
            src_ref=src,
            dst_ref=dst,
            send_sem=send_sem,
            recv_sem=recv_sem,
            device_id={axis: target},
            device_id_type=MESH,
        )
        copy.start()
        pending.append(copy)
        return copy

    gain = 1.0 / (math.log(2.0) * dp * temper)
    if in_line(points, nlst):
        settle, points_of, place = line_gather(s, lst, gain, loads, arrive)
    else:
        settle, points_of, place = any_gather(
            s, nlst, npts, lst, pts, send, chunks, gain, loads, arrive
        )

    def lane_dense(sums):
        return jnp.sum(sums.T, axis=0, keepdims=True)

    row_scale = None
    for sweep in range(ITERS):
        if sweep == 0:

            @pl.loop(0, list_blocks, unroll=4)
            def _(b):
                s.dense[pl.ds(b, 1), :] = lane_dense(s.lane_sums[block(b, LANES), :])
        else:
            wide = [
                jnp.broadcast_to(row_scale[m : m + 1, :], (16, LANES)).astype(BF16)
                for m in range(point_blocks)
            ]

            @pl.loop(0, list_blocks, unroll=4)
            def _(b, wide=wide):
                groups = []
                for q in range(LANES // 16):
                    rows = block(b * (LANES // 16) + q, 16)
                    groups.append(
                        added(
                            [
                                s.energy[rows, m * LANES : (m + 1) * LANES] * wide[m]
                                for m in range(point_blocks)
                            ]
                        )
                    )
                s.dense[pl.ds(b, 1), :] = lane_dense(jnp.concatenate(groups, axis=0).astype(F32))

        s.col_sums[sweep, 0] = s.dense[...].astype(BF16)
        copies = [
            send(
                s.col_sums.at[sweep, 0],
                s.col_sums.at[sweep, d],
                s.c_send.at[sweep, d],
                s.c_recv.at[sweep, d],
                "pts",
                (pts + d) % npts,
            )
            for d in range(1, npts)
        ]
        for copy in copies:
            copy.wait_recv()
        total = added([s.col_sums[sweep, d].astype(F32) for d in range(npts)])
        s.dense[...] = balance / total

        def row_step(b, acc):
            rows = block(b, LANES)
            wide = column_of(s.dense[pl.ds(b, 1), :], LANES).astype(BF16)
            parts = []
            for m in range(point_blocks):
                term = halved(s.energy[rows, m * LANES : (m + 1) * LANES] * wide, 16).astype(F32)
                parts.append(acc[m] + halved(term, 8))
            return tuple(parts)

        acc = lax.fori_loop(
            0,
            list_blocks,
            row_step,
            tuple(jnp.zeros((8, LANES), F32) for _ in range(point_blocks)),
            unroll=4,
        )
        s.row_sums[sweep, 0] = jnp.concatenate(
            [jnp.sum(part, axis=0, keepdims=True) for part in acc], axis=0
        )
        copies = [
            send(
                s.row_sums.at[sweep, 0],
                s.row_sums.at[sweep, d],
                s.r_send.at[sweep, d],
                s.r_recv.at[sweep, d],
                "lst",
                (lst + d) % nlst,
            )
            for d in range(1, nlst)
        ]
        for copy in copies:
            copy.wait_recv()
        row_scale = 1.0 / added([s.row_sums[sweep, d] for d in range(nlst)])
    logs = jnp.log(row_scale)
    for m in range(point_blocks):
        row_log[place[m] : place[m] + 1, :] = logs[m : m + 1, :]

    for m in range(point_blocks):
        wide = column_of(row_scale[m : m + 1, :], LANES)
        values = points_of(m).astype(F32)
        for h in range(dp // LANES):
            lanes = slice(h * LANES, (h + 1) * LANES)
            s.scaled[m * LANES : (m + 1) * LANES, lanes] = (values[:, lanes] * wide).astype(BF16)

    tile = min(512, own)

    def partial_sums(owner, store):
        @pl.loop(0, own // tile)
        def _(t):
            rows = block(owner * (own // tile) + t, tile)
            store(
                block(t, tile),
                jnp.dot(s.energy[rows, :], s.scaled[...], preferred_element_type=F32),
            )

    partner = pts + 1 - 2 * core
    x_copies = []
    order = [d % chips for d in range(1, chips + 1)]
    for d in order:

        def to_pair(rows, values, d=d):
            s.pair_send[d, rows, :] = values.astype(BF16)

        partial_sums(((chip + d) % chips) * 2 + 1 - core, to_pair)
        x_copies.append(
            send(
                s.pair_send.at[d],
                s.pair_recv.at[d],
                s.px_send.at[d],
                s.px_recv.at[d],
                "pts",
                partner,
            )
        )
    y_copies = []
    for n, d in enumerate(order):

        def to_mine(rows, values):
            s.mine[rows, :] = values

        owner = ((chip + d) % chips) * 2 + core
        partial_sums(owner, to_mine)
        x_copies[n].wait_recv()
        pair = s.mine[...] + s.pair_recv[d].astype(F32)
        if d:
            s.chip_send[d] = pair.astype(BF16)
            y_copies.append(
                send(
                    s.chip_send.at[d],
                    s.chip_recv.at[d],
                    s.py_send.at[d],
                    s.py_recv.at[d],
                    "pts",
                    owner,
                )
            )
        else:
            s.mine[...] = pair
    for copy in y_copies:
        copy.wait_recv()
    for j in range(own // LANES):
        rows = slice(j * LANES, (j + 1) * LANES)
        sums = s.mine[rows, :]
        for d in range(1, chips):
            sums += s.chip_recv[d, rows, :].astype(F32)
        wide = column_of(s.dense[pl.ds(pts * (own // LANES) + j, 1), :], LANES)
        out[rows, :] = rms_norm(sums * jnp.concatenate([wide] * (dp // LANES), axis=1))
    for copy in pending:
        copy.wait_send()
    settle()


def in_line(points, nlst):
    return nlst == 4 and points % (2 * LANES) == 0


def on_device(npts, nlst, tower_out, projection, centroids):
    points, feats = tower_out.shape
    lists, dp = centroids.shape
    share = points // nlst
    own = lists // npts
    chips = npts // 2
    chunks = 2 if share % (2 * LANES) == 0 else 1
    vmem = pl.BlockSpec(memory_space=pltpu.VMEM)
    hbm = pl.BlockSpec(memory_space=pl.ANY)
    sem = pltpu.SemaphoreType.DMA
    scratch = dict(
        tower=pltpu.VMEM((points, feats), BF16),
        proj=pltpu.VMEM((feats, dp), BF16),
        unit=pltpu.VMEM((lists, dp), BF16),
        energy=pltpu.VMEM((lists, points), BF16),
        lane_sums=pltpu.VMEM((lists, LANES), F32),
        dense=pltpu.VMEM((lists // LANES, LANES), F32),
        col_sums=pltpu.VMEM((ITERS, npts, lists // LANES, LANES), BF16),
        row_sums=pltpu.VMEM((ITERS, nlst, points // LANES, LANES), F32),
        scaled=pltpu.VMEM((points, dp), BF16),
        pair_send=pltpu.VMEM((chips, own, dp), BF16),
        pair_recv=pltpu.VMEM((chips, own, dp), BF16),
        chip_send=pltpu.VMEM((chips, own, dp), BF16),
        chip_recv=pltpu.VMEM((chips, own, dp), BF16),
        mine=pltpu.VMEM((own, dp), F32),
        load=sem((3,)),
        c_send=sem((ITERS, npts)),
        c_recv=sem((ITERS, npts)),
        r_send=sem((ITERS, nlst)),
        r_recv=sem((ITERS, nlst)),
        px_send=sem((chips,)),
        px_recv=sem((chips,)),
        py_send=sem((chips,)),
        py_recv=sem((chips,)),
    )
    if in_line(points, nlst):
        scratch.update(line_scratch(points, lists, feats, dp))
    else:
        scratch.update(any_scratch(points, lists, feats, dp, npts, nlst, chunks))
    centers, row_log = pl.pallas_call(
        functools.partial(kernel, npts, nlst, chunks, tuple(scratch)),
        out_shape=(
            jax.ShapeDtypeStruct((own, dp), F32),
            jax.ShapeDtypeStruct((points // LANES, LANES), F32),
        ),
        in_specs=[hbm] * 3,
        out_specs=(vmem, vmem),
        scratch_shapes=list(scratch.values()),
        compiler_params=pltpu.CompilerParams(
            collective_id=0, has_side_effects=True, vmem_limit_bytes=60000000
        ),
    )(tower_out, projection, centroids)
    return centers, row_log.reshape(points)


def solution(mesh):
    return jax.shard_map(
        functools.partial(on_device, mesh.shape["pts"], mesh.shape["lst"]),
        mesh=mesh,
        in_specs=(P("pts", "lst"), P("lst", None), P("lst", None)),
        out_specs=(P(("lst", "pts"), None), P("pts")),
        check_vma=False,
    )
```

time: 113 us -> 108 us (0.956)
  Pallas kernels: 109 us -> 104 us
    pallas_call x1, Pallas kernels: 109 us -> 104 us  [on_device(): pl.pallas_call(functools.partial(kernel, npts, nlst, chunks, tuple(scratc...]
where the time goes in v1:
time: 108 us; the launch traced here: 107 us
  Pallas kernels  104 us (96%)
  local copies, waits for them, and re-layouts  3.16 us (3%)
    pallas_call x1, Pallas kernels, on_device(): pl.pallas_call(functools.partial(kernel, npts, nlst, chunks, tuple(scratc...  104 us
    unnamed x2, local copies, waits for them, and re-layouts  3.16 us

profile of v1, /device:TPU:0, one launch (start us, length us, event | category | flops | bytes accessed | tf_op | source)
XLA Modules:
  0.0 107.4 jit_solution(18445030648759254799)
XLA Ops:
  0.6 103.6 %shard_map.50 = (f32[512,256]{1,0:T(8,128)}, f32[16,128]{1,0:T(8,128)}) custom-call(bf16[2048,256]{1,0:T(8,128)(2,1)} %tower.1, bf16[256,256]{1,0:T(8,128)(2,1)} %proj.1, bf16[4096,256]{1,0:T(8,128)(2,1)} %cent.1), custom_call_target="tpu_custom_call" | custom-call | tf_op jit(solution)/shard_map/pallas_call | solution.py:634
  104.2 1.9 %copy.7 = f32[512,256]{1,0:T(8,128)} copy(f32[512,256]{1,0:T(8,128)} %get-tuple-element.8) | data formatting | bytes 1048576
  106.1 1.3 %copy.8 = f32[2048]{0:T(1024)} copy(f32[2048]{0:T(1024)} %bitcast.1) | data formatting | bytes 16384

commit v2 on v1

--- a/solution.py
+++ b/solution.py
@@ -12,6 +12,7 @@
 ITERS = 3
 temper = 0.05
 LANES = 128
+AHEAD = 2
 MESH = pl.DeviceIdType.MESH
 F32 = jnp.float32
 BF16 = jnp.bfloat16
@@ -112,27 +113,33 @@
     loads["tower"].wait()
     arrive()
 
-    @pl.loop(0, steps)
+    def partial(h, t):
+        values = jnp.dot(
+            s.tower[block(h * steps + t, LANES), :], s.proj[...], preferred_element_type=F32
+        )
+
+        @pl.when(outer)
+        def _():
+            s.part[h, t] = values.astype(BF16)
+            feed(h, t).start()
+
+        @pl.when(inner)
+        def _():
+            s.own[h, t] = values
+
+    @pl.loop(0, steps + AHEAD)
     def _(t):
-        for h in (far, near):
-            values = jnp.dot(
-                s.tower[block(h * steps + t, LANES), :], s.proj[...], preferred_element_type=F32
-            )
-
-            @pl.when(outer)
-            def _(h=h, values=values):
-                s.part[h, t] = values.astype(BF16)
-                feed(h, t).start()
-
-            @pl.when(inner)
-            def _(h=h, values=values):
-                s.own[h, t] = values
-
-    loads["cent"].wait()
-    unit_lists(s)
+        @pl.when(t < steps)
+        def _():
+            partial(far, t)
+
+        @pl.when(t >= AHEAD)
+        def _():
+            partial(near, t - AHEAD)
+
     e_rows = min(2048, lists)
 
-    @pl.loop(0, steps + 2)
+    @pl.loop(0, steps + AHEAD + 1)
     def _(t):
         @pl.when(inner & (t < steps))
         def _():
@@ -140,9 +147,9 @@
             s.part[far, t] = (s.own[far, t] + s.fed[far, t].astype(F32)).astype(BF16)
             cross(t).start()
 
-        @pl.when(inner & (t >= 1) & (t <= steps))
-        def _():
-            u = t - 1
+        @pl.when(inner & (t >= AHEAD) & (t < steps + AHEAD))
+        def _():
+            u = t - AHEAD
             feed(near, u).wait_recv()
             cross(u).wait_recv()
             hidden = s.own[near, u] + s.fed[near, u].astype(F32) + s.crossed[u].astype(F32)
@@ -150,9 +157,14 @@
             back(u, near).start()
             across(u).start()
 
-        @pl.when(t >= 2)
-        def _():
-            u = t - 2
+        @pl.when(t == 1)
+        def _():
+            loads["cent"].wait()
+            unit_lists(s)
+
+        @pl.when(t > AHEAD)
+        def _():
+            u = t - AHEAD - 1
 
             @pl.when(inner)
             def _():
@@ -407,8 +419,8 @@
 
     pending = []
 
-    def send(src, dst, send_sem, recv_sem, axis, target):
-        copy = pltpu.make_async_remote_copy(
+    def remote(src, dst, send_sem, recv_sem, axis, target):
+        return pltpu.make_async_remote_copy(
             src_ref=src,
             dst_ref=dst,
             send_sem=send_sem,
@@ -416,6 +428,9 @@
             device_id={axis: target},
             device_id_type=MESH,
         )
+
+    def send(*what):
+        copy = remote(*what)
         copy.start()
         pending.append(copy)
         return copy
@@ -431,21 +446,76 @@
     def lane_dense(sums):
         return jnp.sum(sums.T, axis=0, keepdims=True)
 
-    row_scale = None
-    for sweep in range(ITERS):
-        if sweep == 0:
+    @pl.loop(0, list_blocks, unroll=4)
+    def _(b):
+        s.dense[pl.ds(b, 1), :] = lane_dense(s.lane_sums[block(b, LANES), :])
+
+    @pl.loop(0, ITERS)
+    def _(sweep):
+        s.col_sums[sweep, 0] = s.dense[...].astype(BF16)
+        c_copies = [
+            remote(
+                s.col_sums.at[sweep, 0],
+                s.col_sums.at[sweep, d],
+                s.c_send.at[sweep, d],
+                s.c_recv.at[sweep, d],
+                "pts",
+                (pts + d) % npts,
+            )
+            for d in range(1, npts)
+        ]
+        for copy in c_copies:
+            copy.start()
+        for copy in c_copies:
+            copy.wait_recv()
+        total = added([s.col_sums[sweep, d].astype(F32) for d in range(npts)])
+        s.dense[...] = balance / total
+
+        def row_step(b, acc):
+            rows = block(b, LANES)
+            wide = column_of(s.dense[pl.ds(b, 1), :], LANES).astype(BF16)
+            parts = []
+            for m in range(point_blocks):
+                term = halved(s.energy[rows, m * LANES : (m + 1) * LANES] * wide, 16).astype(F32)
+                parts.append(acc[m] + halved(term, 8))
+            return tuple(parts)
+
+        acc = lax.fori_loop(
+            0,
+            list_blocks,
+            row_step,
+            tuple(jnp.zeros((8, LANES), F32) for _ in range(point_blocks)),
+            unroll=4,
+        )
+        s.row_sums[sweep, 0] = jnp.concatenate(
+            [jnp.sum(part, axis=0, keepdims=True) for part in acc], axis=0
+        )
+        r_copies = [
+            remote(
+                s.row_sums.at[sweep, 0],
+                s.row_sums.at[sweep, d],
+                s.r_send.at[sweep, d],
+                s.r_recv.at[sweep, d],
+                "lst",
+                (lst + d) % nlst,
+            )
+            for d in range(1, nlst)
+        ]
+        for copy in r_copies:
+            copy.start()
+        for copy in r_copies:
+            copy.wait_recv()
+        s.row_scale[...] = 1.0 / added([s.row_sums[sweep, d] for d in range(nlst)])
+
+        @pl.when(sweep < ITERS - 1)
+        def _():
+            wide = [
+                jnp.broadcast_to(s.row_scale[m : m + 1, :], (16, LANES)).astype(BF16)
+                for m in range(point_blocks)
+            ]
 
             @pl.loop(0, list_blocks, unroll=4)
             def _(b):
-                s.dense[pl.ds(b, 1), :] = lane_dense(s.lane_sums[block(b, LANES), :])
-        else:
-            wide = [
-                jnp.broadcast_to(row_scale[m : m + 1, :], (16, LANES)).astype(BF16)
-                for m in range(point_blocks)
-            ]
-
-            @pl.loop(0, list_blocks, unroll=4)
-            def _(b, wide=wide):
                 groups = []
                 for q in range(LANES // 16):
                     rows = block(b * (LANES // 16) + q, 16)
@@ -459,56 +529,10 @@
                     )
                 s.dense[pl.ds(b, 1), :] = lane_dense(jnp.concatenate(groups, axis=0).astype(F32))
 
-        s.col_sums[sweep, 0] = s.dense[...].astype(BF16)
-        copies = [
-            send(
-                s.col_sums.at[sweep, 0],
-                s.col_sums.at[sweep, d],
-                s.c_send.at[sweep, d],
-                s.c_recv.at[sweep, d],
-                "pts",
-                (pts + d) % npts,
-            )
-            for d in range(1, npts)
-        ]
-        for copy in copies:
-            copy.wait_recv()
-        total = added([s.col_sums[sweep, d].astype(F32) for d in range(npts)])
-        s.dense[...] = balance / total
-
-        def row_step(b, acc):
-            rows = block(b, LANES)
-            wide = column_of(s.dense[pl.ds(b, 1), :], LANES).astype(BF16)
-            parts = []
-            for m in range(point_blocks):
-                term = halved(s.energy[rows, m * LANES : (m + 1) * LANES] * wide, 16).astype(F32)
-                parts.append(acc[m] + halved(term, 8))
-            return tuple(parts)
-
-        acc = lax.fori_loop(
-            0,
-            list_blocks,
-            row_step,
-            tuple(jnp.zeros((8, LANES), F32) for _ in range(point_blocks)),
-            unroll=4,
-        )
-        s.row_sums[sweep, 0] = jnp.concatenate(
-            [jnp.sum(part, axis=0, keepdims=True) for part in acc], axis=0
-        )
-        copies = [
-            send(
-                s.row_sums.at[sweep, 0],
-                s.row_sums.at[sweep, d],
-                s.r_send.at[sweep, d],
-                s.r_recv.at[sweep, d],
-                "lst",
-                (lst + d) % nlst,
-            )
-            for d in range(1, nlst)
-        ]
-        for copy in copies:
-            copy.wait_recv()
-        row_scale = 1.0 / added([s.row_sums[sweep, d] for d in range(nlst)])
+        for copy in c_copies + r_copies:
+            copy.wait_send()
+
+    row_scale = s.row_scale[...]
     logs = jnp.log(row_scale)
     for m in range(point_blocks):
         row_log[place[m] : place[m] + 1, :] = logs[m : m + 1, :]
@@ -522,60 +546,69 @@
 
     tile = min(512, own)
 
-    def partial_sums(owner, store):
+    def chip_at(d):
+        if chips == 4:
+            return (chip // 2 + d // 2) % 2 * 2 + (chip + d) % 2
+        return (chip + d) % chips
+
+    def to_pair(d):
+        return remote(
+            s.pair_send.at[d],
+            s.pair_recv.at[d],
+            s.px_send.at[d],
+            s.px_recv.at[d],
+            "pts",
+            pts + 1 - 2 * core,
+        )
+
+    def to_chip(d):
+        return remote(
+            s.chip_send.at[d],
+            s.chip_recv.at[d],
+            s.py_send.at[d],
+            s.py_recv.at[d],
+            "pts",
+            chip_at(d) * 2 + core,
+        )
+
+    last = 2 * chips - 1
+
+    @pl.loop(0, 2 * chips)
+    def _(k):
+        for_pair = (k == 0) | ((k % 2 == 1) & (k < last))
+        turn = jnp.where(for_pair, (k + 1) // 2, jnp.where(k == last, chips - 1, k // 2 - 1))
+        d = chips - 1 - turn
+        owner = chip_at(d) * 2 + jnp.where(for_pair, 1 - core, core)
+
         @pl.loop(0, own // tile)
         def _(t):
-            rows = block(owner * (own // tile) + t, tile)
-            store(
-                block(t, tile),
-                jnp.dot(s.energy[rows, :], s.scaled[...], preferred_element_type=F32),
+            s.mine[block(t, tile), :] = jnp.dot(
+                s.energy[block(owner * (own // tile) + t, tile), :],
+                s.scaled[...],
+                preferred_element_type=F32,
             )
 
-    partner = pts + 1 - 2 * core
-    x_copies = []
-    order = [d % chips for d in range(1, chips + 1)]
-    for d in order:
-
-        def to_pair(rows, values, d=d):
-            s.pair_send[d, rows, :] = values.astype(BF16)
-
-        partial_sums(((chip + d) % chips) * 2 + 1 - core, to_pair)
-        x_copies.append(
-            send(
-                s.pair_send.at[d],
-                s.pair_recv.at[d],
-                s.px_send.at[d],
-                s.px_recv.at[d],
-                "pts",
-                partner,
-            )
-        )
-    y_copies = []
-    for n, d in enumerate(order):
-
-        def to_mine(rows, values):
-            s.mine[rows, :] = values
-
-        owner = ((chip + d) % chips) * 2 + core
-        partial_sums(owner, to_mine)
-        x_copies[n].wait_recv()
-        pair = s.mine[...] + s.pair_recv[d].astype(F32)
-        if d:
-            s.chip_send[d] = pair.astype(BF16)
-            y_copies.append(
-                send(
-                    s.chip_send.at[d],
-                    s.chip_recv.at[d],
-                    s.py_send.at[d],
-                    s.py_recv.at[d],
-                    "pts",
-                    owner,
-                )
-            )
-        else:
-            s.mine[...] = pair
-    for copy in y_copies:
-        copy.wait_recv()
+        @pl.when(for_pair)
+        def _():
+            s.pair_send[d] = s.mine[...].astype(BF16)
+            to_pair(d).start()
+
+        @pl.when(jnp.logical_not(for_pair))
+        def _():
+            to_pair(d).wait_recv()
+            both = s.mine[...] + s.pair_recv[d].astype(F32)
+
+            @pl.when(d > 0)
+            def _():
+                s.chip_send[d] = both.astype(BF16)
+                to_chip(d).start()
+
+            @pl.when(d == 0)
+            def _():
+                s.mine[...] = both
+
+    for d in range(1, chips):
+        to_chip(d).wait_recv()
     for j in range(own // LANES):
         rows = slice(j * LANES, (j + 1) * LANES)
         sums = s.mine[rows, :]
@@ -585,6 +618,10 @@
         out[rows, :] = rms_norm(sums * jnp.concatenate([wide] * (dp // LANES), axis=1))
     for copy in pending:
         copy.wait_send()
+    for d in range(chips):
+        to_pair(d).wait_send()
+    for d in range(1, chips):
+        to_chip(d).wait_send()
     settle()
 
 
@@ -608,6 +645,7 @@
         unit=pltpu.VMEM((lists, dp), BF16),
         energy=pltpu.VMEM((lists, points), BF16),
         lane_sums=pltpu.VMEM((lists, LANES), F32),
+        row_scale=pltpu.VMEM((points // LANES, LANES), F32),
         dense=pltpu.VMEM((lists // LANES, LANES), F32),
         col_sums=pltpu.VMEM((ITERS, npts, lists // LANES, LANES), BF16),
         row_sums=pltpu.VMEM((ITERS, nlst, points // LANES, LANES), F32),

time: 108 us -> 104 us (0.963)
  Pallas kernels: 104 us -> 99.9 us
    pallas_call x1, Pallas kernels: 104 us -> 99.9 us  [on_device(): pl.pallas_call(functools.partial(kernel, npts, nlst, chunks, tuple(scratc...]
where the time goes in v2:
time: 104 us
  Pallas kernels  99.9 us (96%)
  local copies, waits for them, and re-layouts  3.16 us (3%)
    pallas_call x1, Pallas kernels, on_device(): pl.pallas_call(functools.partial(kernel, npts, nlst, chunks, tuple(scratc...  99.9 us
    unnamed x2, local copies, waits for them, and re-layouts  3.16 us

profile of v2, /device:TPU:0, one launch (start us, length us, event | category | flops | bytes accessed | tf_op | source)
XLA Modules:
  0.0 103.7 jit_solution(17686466552029595077)
XLA Ops:
  0.6 99.9 %shard_map.50 = (f32[512,256]{1,0:T(8,128)}, f32[16,128]{1,0:T(8,128)}) custom-call(bf16[2048,256]{1,0:T(8,128)(2,1)} %tower.1, bf16[256,256]{1,0:T(8,128)(2,1)} %proj.1, bf16[4096,256]{1,0:T(8,128)(2,1)} %cent.1), custom_call_target="tpu_custom_call" | custom-call | tf_op jit(solution)/shard_map/pallas_call | solution.py:672
  100.5 1.9 %copy.7 = f32[512,256]{1,0:T(8,128)} copy(f32[512,256]{1,0:T(8,128)} %get-tuple-element.8) | data formatting | bytes 1048576
  102.4 1.3 %copy.8 = f32[2048]{0:T(1024)} copy(f32[2048]{0:T(1024)} %bitcast.1) | data formatting | bytes 16384

commit v3 on v2

--- a/solution.py
+++ b/solution.py
@@ -24,13 +24,6 @@
 
 def column_of(row, rows):
     return jnp.broadcast_to(row, (rows, LANES)).T
-
-
-def halved(values, rows):
-    while values.shape[0] > rows:
-        n = values.shape[0] // 2
-        values = values[:n] + values[n:]
-    return values
 
 
 def added(terms):
@@ -471,24 +464,20 @@
         total = added([s.col_sums[sweep, d].astype(F32) for d in range(npts)])
         s.dense[...] = balance / total
 
-        def row_step(b, acc):
-            rows = block(b, LANES)
-            wide = column_of(s.dense[pl.ds(b, 1), :], LANES).astype(BF16)
-            parts = []
-            for m in range(point_blocks):
-                term = halved(s.energy[rows, m * LANES : (m + 1) * LANES] * wide, 16).astype(F32)
-                parts.append(acc[m] + halved(term, 8))
-            return tuple(parts)
-
-        acc = lax.fori_loop(
-            0,
-            list_blocks,
-            row_step,
-            tuple(jnp.zeros((8, LANES), F32) for _ in range(point_blocks)),
-            unroll=4,
-        )
+        depth = min(512, lists)
+        acc = jnp.zeros((16, points), F32)
+        for b in range(lists // depth):
+            scales = [
+                jnp.broadcast_to(s.dense[k : k + 1, :], (16, LANES)).astype(BF16)
+                for k in range(b * (depth // LANES), (b + 1) * (depth // LANES))
+            ]
+            acc += jnp.dot(
+                jnp.concatenate(scales, axis=1),
+                s.energy[b * depth : (b + 1) * depth, :],
+                preferred_element_type=F32,
+            )
         s.row_sums[sweep, 0] = jnp.concatenate(
-            [jnp.sum(part, axis=0, keepdims=True) for part in acc], axis=0
+            [acc[0:1, m * LANES : (m + 1) * LANES] for m in range(point_blocks)], axis=0
         )
         r_copies = [
             remote(

time: 104 us -> 98.5 us (0.947)
  Pallas kernels: 99.9 us -> 94.5 us
    pallas_call x1, Pallas kernels: 99.9 us -> 94.5 us  [on_device(): pl.pallas_call(functools.partial(kernel, npts, nlst, chunks, tuple(scratc...]
where the time goes in v3:
time: 98.5 us; the launch traced here: 98.3 us
  Pallas kernels  94.5 us (96%)
  local copies, waits for them, and re-layouts  3.16 us (3%)
    pallas_call x1, Pallas kernels, on_device(): pl.pallas_call(functools.partial(kernel, npts, nlst, chunks, tuple(scratc...  94.5 us
    unnamed x2, local copies, waits for them, and re-layouts  3.16 us

profile of v3, /device:TPU:0, one launch (start us, length us, event | category | flops | bytes accessed | tf_op | source)
XLA Modules:
  0.0 98.3 jit_solution(11600865718307252733)
XLA Ops:
  0.6 94.5 %shard_map.50 = (f32[512,256]{1,0:T(8,128)}, f32[16,128]{1,0:T(8,128)}) custom-call(bf16[2048,256]{1,0:T(8,128)(2,1)} %tower.1, bf16[256,256]{1,0:T(8,128)(2,1)} %proj.1, bf16[4096,256]{1,0:T(8,128)(2,1)} %cent.1), custom_call_target="tpu_custom_call" | custom-call | tf_op jit(solution)/shard_map/pallas_call | solution.py:661
  95.1 1.9 %copy.7 = f32[512,256]{1,0:T(8,128)} copy(f32[512,256]{1,0:T(8,128)} %get-tuple-element.8) | data formatting | bytes 1048576
  97.0 1.3 %copy.8 = f32[2048]{0:T(1024)} copy(f32[2048]{0:T(1024)} %bitcast.1) | data formatting | bytes 16384

commit v4 on v3

--- a/solution.py
+++ b/solution.py
@@ -436,12 +436,18 @@
             s, nlst, npts, lst, pts, send, chunks, gain, loads, arrive
         )
 
+    ones = jnp.ones((LANES, LANES), BF16)
+    diagonal = lax.broadcasted_iota(jnp.int32, (LANES, LANES), 0) == lax.broadcasted_iota(
+        jnp.int32, (LANES, LANES), 1
+    )
+
     def lane_dense(sums):
-        return jnp.sum(sums.T, axis=0, keepdims=True)
+        wide = jnp.dot(sums, ones, preferred_element_type=F32)
+        return jnp.sum(jnp.where(diagonal, wide, 0.0), axis=0, keepdims=True)
 
     @pl.loop(0, list_blocks, unroll=4)
     def _(b):
-        s.dense[pl.ds(b, 1), :] = lane_dense(s.lane_sums[block(b, LANES), :])
+        s.dense[pl.ds(b, 1), :] = lane_dense(s.lane_sums[block(b, LANES), :].astype(BF16))
 
     @pl.loop(0, ITERS)
     def _(sweep):
@@ -516,7 +522,7 @@
                             ]
                         )
                     )
-                s.dense[pl.ds(b, 1), :] = lane_dense(jnp.concatenate(groups, axis=0).astype(F32))
+                s.dense[pl.ds(b, 1), :] = lane_dense(jnp.concatenate(groups, axis=0))
 
         for copy in c_copies + r_copies:
             copy.wait_send()

time: 98.5 us -> 99.5 us (1.010)
  no operation moved by 1% of the time
where the time goes in v4:
time: 99.5 us; the launch traced here: 99.2 us
  Pallas kernels  95.4 us (96%)
  local copies, waits for them, and re-layouts  3.16 us (3%)
    pallas_call x1, Pallas kernels, on_device(): pl.pallas_call(functools.partial(kernel, npts, nlst, chunks, tuple(scratc...  95.4 us
    unnamed x2, local copies, waits for them, and re-layouts  3.16 us

profile of v4, /device:TPU:0, one launch (start us, length us, event | category | flops | bytes accessed | tf_op | source)
XLA Modules:
  0.0 99.2 jit_solution(5687154024381988194)
XLA Ops:
  0.6 95.4 %shard_map.50 = (f32[512,256]{1,0:T(8,128)}, f32[16,128]{1,0:T(8,128)}) custom-call(bf16[2048,256]{1,0:T(8,128)(2,1)} %tower.1, bf16[256,256]{1,0:T(8,128)(2,1)} %proj.1, bf16[4096,256]{1,0:T(8,128)(2,1)} %cent.1), custom_call_target="tpu_custom_call" | custom-call | tf_op jit(solution)/shard_map/pallas_call | solution.py:667
  96.1 1.9 %copy.7 = f32[512,256]{1,0:T(8,128)} copy(f32[512,256]{1,0:T(8,128)} %get-tuple-element.8) | data formatting | bytes 1048576
  98.0 1.3 %copy.8 = f32[2048]{0:T(1024)} copy(f32[2048]{0:T(1024)} %bitcast.1) | data formatting | bytes 16384

commit v5 on v3

--- a/solution.py
+++ b/solution.py
@@ -439,7 +439,7 @@
     def lane_dense(sums):
         return jnp.sum(sums.T, axis=0, keepdims=True)
 
-    @pl.loop(0, list_blocks, unroll=4)
+    @pl.loop(0, list_blocks, unroll=8)
     def _(b):
         s.dense[pl.ds(b, 1), :] = lane_dense(s.lane_sums[block(b, LANES), :])
 
@@ -503,7 +503,7 @@
                 for m in range(point_blocks)
             ]
 
-            @pl.loop(0, list_blocks, unroll=4)
+            @pl.loop(0, list_blocks, unroll=8)
             def _(b):
                 groups = []
                 for q in range(LANES // 16):

time: 98.5 us -> 97.5 us (0.990)
  Pallas kernels: 94.5 us -> 93.5 us
where the time goes in v5:
time: 97.5 us; the launch traced here: 97.3 us
  Pallas kernels  93.5 us (96%)
  local copies, waits for them, and re-layouts  3.16 us (3%)
    pallas_call x1, Pallas kernels, on_device(): pl.pallas_call(functools.partial(kernel, npts, nlst, chunks, tuple(scratc...  93.5 us
    unnamed x2, local copies, waits for them, and re-layouts  3.16 us

profile of v5, /device:TPU:0, one launch (start us, length us, event | category | flops | bytes accessed | tf_op | source)
XLA Modules:
  0.0 97.3 jit_solution(13966044359825551376)
XLA Ops:
  0.6 93.5 %shard_map.50 = (f32[512,256]{1,0:T(8,128)}, f32[16,128]{1,0:T(8,128)}) custom-call(bf16[2048,256]{1,0:T(8,128)(2,1)} %tower.1, bf16[256,256]{1,0:T(8,128)(2,1)} %proj.1, bf16[4096,256]{1,0:T(8,128)(2,1)} %cent.1), custom_call_target="tpu_custom_call" | custom-call | tf_op jit(solution)/shard_map/pallas_call | solution.py:661
  94.1 1.9 %copy.7 = f32[512,256]{1,0:T(8,128)} copy(f32[512,256]{1,0:T(8,128)} %get-tuple-element.8) | data formatting | bytes 1048576
  96.0 1.3 %copy.8 = f32[2048]{0:T(1024)} copy(f32[2048]{0:T(1024)} %bitcast.1) | data formatting | bytes 16384

commit v6 on v5

--- a/solution.py
+++ b/solution.py
@@ -130,7 +130,7 @@
         def _():
             partial(near, t - AHEAD)
 
-    e_rows = min(2048, lists)
+    e_rows = min(4096, lists)
 
     @pl.loop(0, steps + AHEAD + 1)
     def _(t):
@@ -439,7 +439,7 @@
     def lane_dense(sums):
         return jnp.sum(sums.T, axis=0, keepdims=True)
 
-    @pl.loop(0, list_blocks, unroll=8)
+    @pl.loop(0, list_blocks, unroll=min(16, list_blocks))
     def _(b):
         s.dense[pl.ds(b, 1), :] = lane_dense(s.lane_sums[block(b, LANES), :])
 
@@ -503,7 +503,7 @@
                 for m in range(point_blocks)
             ]
 
-            @pl.loop(0, list_blocks, unroll=8)
+            @pl.loop(0, list_blocks, unroll=min(16, list_blocks))
             def _(b):
                 groups = []
                 for q in range(LANES // 16):

time: 97.5 us -> 96.4 us (0.989)
  Pallas kernels: 93.5 us -> 92.4 us
    pallas_call x1, Pallas kernels: 93.5 us -> 92.4 us  [on_device(): pl.pallas_call(functools.partial(kernel, npts, nlst, chunks, tuple(scratc...]
where the time goes in v6:
time: 96.4 us; the launch traced here: 96.2 us
  Pallas kernels  92.4 us (96%)
  local copies, waits for them, and re-layouts  3.16 us (3%)
    pallas_call x1, Pallas kernels, on_device(): pl.pallas_call(functools.partial(kernel, npts, nlst, chunks, tuple(scratc...  92.4 us
    unnamed x2, local copies, waits for them, and re-layouts  3.16 us

profile of v6, /device:TPU:0, one launch (start us, length us, event | category | flops | bytes accessed | tf_op | source)
XLA Modules:
  0.0 96.2 jit_solution(17446245788213984576)
XLA Ops:
  0.6 92.4 %shard_map.50 = (f32[512,256]{1,0:T(8,128)}, f32[16,128]{1,0:T(8,128)}) custom-call(bf16[2048,256]{1,0:T(8,128)(2,1)} %tower.1, bf16[256,256]{1,0:T(8,128)(2,1)} %proj.1, bf16[4096,256]{1,0:T(8,128)(2,1)} %cent.1), custom_call_target="tpu_custom_call" | custom-call | tf_op jit(solution)/shard_map/pallas_call | solution.py:661
  93.1 1.9 %copy.7 = f32[512,256]{1,0:T(8,128)} copy(f32[512,256]{1,0:T(8,128)} %get-tuple-element.8) | data formatting | bytes 1048576
  94.9 1.3 %copy.8 = f32[2048]{0:T(1024)} copy(f32[2048]{0:T(1024)} %bitcast.1) | data formatting | bytes 16384
